TPU v7x, 256 devices: a whole 4x4x8 slice. The times are simulated.
256 devices in a mesh: tm: 64 (over y, z_hi, x), neur: 4 (over z_lo, core).
Axes of the slice: x: 4, y: 4, z: 8 (z_hi: 4, z_lo: 2; z = z_hi * 2 + z_lo), core: 2. Of those that a mesh axis runs over, the one named last changes fastest.
Arguments:
- recording: bfloat16 [2048, 16384], P('neur', 'tm'), may hold values from -6 to 6
- motifs: bfloat16 [128, 64, 2048], P(None, None, 'neur'), may hold values from -0.0625 to 0.0625
- loadings: bfloat16 [64, 16384], P(None, 'tm'), may hold values from -6 to 6
Outputs:
- grad_motifs: float32 [128, 64, 2048], P('tm', None, 'neur')
- grad_loadings: float32 [64, 16384], P(None, 'tm')
All inputs are finite; a program needn't handle non-finite values.
Results may differ from a plain program's by a relative error of at most 0.0021.
Values may be sent and summed in bfloat16 or wider, within the bound.
A program may use at most 128 MiB of HBM per device.

v0:
```python
import math
import jax
import jax.numpy as jnp
from jax import lax
from jax.sharding import PartitionSpec as P


def from_behind(block, axis, distance):
    devices = range(lax.axis_size(axis))
    route = [(i - distance, i) for i in devices if i - distance in devices]
    return lax.ppermute(block, axis, route)


def correlate(lhs, rhs, specs):
    return lax.conv_general_dilated(
        lhs, rhs, (1,), "VALID", dimension_numbers=specs, preferred_element_type=jnp.float32
    )


def forward_model(motifs, load_ext, time_len):
    reversed_load = load_ext[:, ::-1]
    result = correlate(reversed_load[None], motifs, ("NCH", "HIO", "NCH"))
    return result[0, :, :time_len][:, ::-1]


def backward_motif(motifs, res_ext, out_len):
    result = correlate(res_ext[None], motifs, ("NCH", "HOI", "NCH"))
    return result[0, :, :out_len]


def weight_term(reversed_load, reversed_res, piece_count):
    time_len = reversed_res.shape[1]
    window = lax.slice_in_dim(reversed_load, 0, piece_count + time_len - 1, axis=1)
    return correlate(window[:, None, :], reversed_res[:, None, :], ("NCH", "OIH", "HNC"))


def on_device(recording, motifs, loadings):
    lag_count = motifs.shape[0]
    motif_count = motifs.shape[1]
    neur_local = recording.shape[0]
    time_len = recording.shape[1]
    tm_count = lax.axis_size("tm")
    lag_share = lag_count // tm_count
    total_time = time_len * tm_count
    neurons = neur_local * lax.axis_size("neur")
    edge_cols = from_behind(loadings[:, time_len - lag_count :], "tm", 1)
    load_ext = jnp.concatenate([edge_cols, loadings], axis=1)
    rebuilt = forward_model(motifs, load_ext, time_len)
    residual = (rebuilt - recording.astype(jnp.float32)).astype(jnp.bfloat16)
    ahead_cols = from_behind(residual[:, :lag_count], "tm", -1)
    partial_value = backward_motif(
        motifs, jnp.concatenate([residual, ahead_cols], axis=1), time_len
    )
    grad_loadings = lax.psum(partial_value, "neur") * math.sqrt(motif_count / neurons)
    reversed_load = load_ext[:, ::-1]
    reversed_res = residual[:, ::-1]
    own_rows = lax.psum_scatter(
        weight_term(reversed_load, reversed_res, lag_share * lax.axis_size("tm")),
        "tm",
        scatter_dimension=0,
        tiled=True,
    )
    grad_motifs = own_rows * (1.0 / math.sqrt(total_time))
    return (grad_motifs, grad_loadings)


def solution(mesh):
    in_specs = (P("neur", "tm"), P(None, None, "neur"), P(None, "tm"))
    out_specs = (P("tm", None, "neur"), P(None, "tm"))
    return jax.shard_map(
        on_device, mesh=mesh, in_specs=in_specs, out_specs=out_specs, check_vma=False
    )
```

profile of v0, /device:TPU:0, one launch (start us, length us, event | category | flops | bytes accessed | tf_op | source)
XLA Modules:
  0.0 547.0 jit_solution(15876584063719561310)
XLA Ops:
  8.0 0.0 all-reduce.2.cloned.1.call-start
  8.0 0.7 slice.18
  8.8 1.7 collective-permute-start
  10.4 1.1 copy.6
  11.5 0.3 collective-permute-done
  11.9 0.8 constant_dynamic-update-slice_fusion
  12.6 0.3 rev.10
  12.9 0.1 slice.24
  13.0 0.2 copy.5
  13.2 18.7 %fusion.4 = f32[1,512,256]{1,0,2:T(1,128)S(1)} fusion(bf16[1,64,384]{1,0,2:T(2,128)(2,1)S(1)} %copy.5, bf16[128,64,512]{2,1,0:T(8,128)(2,1)} %param.4), kind=kOutput, calls=%fused_computation.12 | convolution fusion | flops 2147483648 | bytes 8962048 | tf_op jit(solution)/shard_map/slice | solution.py:23
  31.9 0.3 rev.11
  32.2 0.1 subtract_convert_fusion
  32.3 0.3 rev.12
  32.6 0.3 reverse.1
  32.9 1.5 collective-permute-start.1
  34.4 0.1 slice_bitcast_fusion
  34.4 0.2 copy.7
  34.6 5.4 collective-permute-done.1
  40.0 24.7 %fusion = f32[1,64,256]{1,0,2:T(1,128)} fusion(bf16[128,64,512]{2,1,0:T(8,128)(2,1)} %param.4, bf16[1,512,384]{1,2,0:T(8,128)(2,1)S(1)} %maximum_bitcast_fusion), kind=kOutput, calls=%fused_computation | convolution fusion | flops 2147483648 | bytes 8847360 | tf_op jit(solution)/shard_map/slice | solution.py:28
  64.7 0.0 all-reduce.2.cloned.1.call-update
  64.7 0.3 reduce-scatter.2.cloned.1.call-start
  65.0 19.4 %fusion.2 = f32[128,64,512]{2,1,0:T(8,128)} fusion(bf16[64,1,383]{0,1,2:T(2,128)(2,1)S(1)} %copy.7, bf16[512,1,256]{0,2,1:T(8,128)(2,1)S(1)} %bitcast.16), kind=kOutput, calls=%fused_computation.3 | convolution fusion | flops 2147483648 | bytes 17088384 | tf_op jit(solution)/shard_map/conv_general_dilated | solution.py:15
  84.4 0.0 reduce-scatter.2.cloned.1.call-update
  84.4 33.6 %all-reduce.2.cloned.1.call-done = f32[64,256]{0,1:T(8,128)} async-done(((f32[64,256]{0,1:T(8,128)}), f32[64,256]{0,1:T(8,128)}) %all-reduce.2.cloned.1.call-update) | async-done | bytes 65552 | tf_op jit(solution)/shard_map/psum | solution.py:54
  118.0 0.9 broadcast_multiply_fusion.1
  119.0 0.7 copy.10
  119.7 418.2 %reduce-scatter.2.cloned.1.call-done = f32[2,64,512]{2,1,0:T(8,128)} async-done(((f32[128,64,512]{2,1,0:T(8,128)}), f32[2,64,512]{2,1,0:T(8,128)}) %reduce-scatter.2.cloned.1.call-update) | async-done | bytes 262160 | tf_op jit(solution)/shard_map/reduce_scatter | solution.py:57
  537.9 1.7 broadcast_multiply_fusion
  (4 shorter events, 0.1 us)
Async XLA Ops:
  8.0 110.0 %all-reduce.2.cloned.1.call-start = ((), (), s32[]{:S(2)}) async-start(), calls=%async_computation.2 | async-start | bytes 262144 | tf_op jit(solution)/shard_map/psum | solution.py:54
  8.8 3.1 collective-permute-start
  32.9 7.1 %collective-permute-start.1 = (bf16[512,128]{0,1:T(8,128)(2,1)S(1)}, bf16[512,128]{0,1:T(8,128)(2,1)S(1)}, u32[]{:S(2)}, u32[]{:S(2)}) collective-permute-start(bf16[512,128]{0,1:T(8,128)(2,1)S(1)} %slice.25), channel_id=1, source_target_pairs={{4,0},{8,4},{12,8},{16,12},{20,16},{24,20},{28,24},{32,28},{36,32}... | collective-permute-start | bytes 393224 | tf_op jit(solution)/shard_map/ppermute | solution.py:11
  64.7 473.1 %reduce-scatter.2.cloned.1.call-start = ((), (), s32[]{:S(2)}) async-start(), calls=%async_computation.1 | async-start | bytes 17039360 | tf_op jit(solution)/shard_map/reduce_scatter | solution.py:57
Sparse Core Ops, SparseCore 0:
  64.9 53.1 all-reduce.1
Sparse Core Ops, SparseCore 1:
  84.5 453.3 reduce-scatter.1
where the time goes:
time: 547 us
  waiting for transfers between devices  458 us (84%)
  matrix products  62.7 us (11%)
  between operations  15.6 us (3%)
    reduce_scatter x1, waiting for transfers between devices, on_device(): lax.psum_scatter(weight_term(reversed_load, reversed_res, lag_share * lax...  418 us
    psum x1, waiting for transfers between devices, on_device(): lax.psum(partial_value, 'neur') * math.sqrt(motif_count / neurons)  33.6 us
    slice x1, matrix products, backward_motif(): return result[0, :, :out_len]  24.7 us
    conv_general_dilated x1, matrix products, correlate(): lax.conv_general_dilated(lhs, rhs, (1,), 'VALID', dimension_numbers=specs...  19.4 us
    slice x1, matrix products, forward_model(): return result[0, :, :time_len][:, ::-1]  18.7 us
  transfers between devices with their start and end apart: 4, of which 4 were waited for; matrix products, arithmetic and copies ran while one was open for 4% of the time, Pallas kernels for 0%

commit v1 on v0

--- a/solution.py
+++ b/solution.py
@@ -51,7 +51,12 @@
     partial_value = backward_motif(
         motifs, jnp.concatenate([residual, ahead_cols], axis=1), time_len
     )
-    grad_loadings = lax.psum(partial_value, "neur") * math.sqrt(motif_count / neurons)
+
+    def do_the_figure(payload, axis_tag):
+        piece_next = lax.all_gather(payload, axis_name=axis_tag).sum(axis=0)
+        return piece_next
+
+    grad_loadings = do_the_figure(partial_value, "neur") * math.sqrt(motif_count / neurons)
     reversed_load = load_ext[:, ::-1]
     reversed_res = residual[:, ::-1]
     own_rows = lax.psum_scatter(

time: 547 us -> 517 us (0.945)
  waiting for transfers between devices: 458 us -> 416 us
  blocking collectives: 0 us -> 13.1 us
    psum x1 -> x0, waiting for transfers between devices: 33.6 us -> none  [on_device(): lax.psum(partial_value, 'neur') * math.sqrt(motif_count / neurons)]
    all_gather x0 -> x1, blocking collectives: none -> 13.1 us  [do_the_figure(): piece_next = lax.all_gather(payload, axis_name=axis_tag).sum(axis=0)]
    reduce_scatter x1, waiting for transfers between devices: 418 us -> 410 us  [on_device(): lax.psum_scatter(weight_term(reversed_load, reversed_res, lag_share * lax...]
  transfers between devices with their start and end apart: 4 -> 3, of which waited for: 4 -> 3; matrix products, arithmetic and copies ran while one was open for 4% -> 5% of each run, Pallas kernels for 0% -> 0%
where the time goes in v1:
time: 517 us
  waiting for transfers between devices  416 us (80%)
  matrix products  62.3 us (12%)
  between operations  14.2 us (3%)
  blocking collectives  13.1 us (3%)
  local copies, waits for them, and re-layouts  6.3 us (1%)
    reduce_scatter x1, waiting for transfers between devices, on_device(): lax.psum_scatter(weight_term(reversed_load, reversed_res, lag_share * lax...  410 us
    slice x1, matrix products, backward_motif(): return result[0, :, :out_len]  24 us
    conv_general_dilated x1, matrix products, correlate(): lax.conv_general_dilated(lhs, rhs, (1,), 'VALID', dimension_numbers=specs...  19.6 us
    slice x1, matrix products, forward_model(): return result[0, :, :time_len][:, ::-1]  18.7 us
    all_gather x1, blocking collectives, do_the_figure(): piece_next = lax.all_gather(payload, axis_name=axis_tag).sum(axis=0)  13.1 us
  transfers between devices with their start and end apart: 3, of which 3 were waited for; matrix products, arithmetic and copies ran while one was open for 5% of the time, Pallas kernels for 0%

profile of v1, /device:TPU:0, one launch (start us, length us, event | category | flops | bytes accessed | tf_op | source)
XLA Modules:
  0.0 516.7 jit_solution(16834507838326234762)
XLA Ops:
  7.2 0.0 reduce-scatter.2.cloned.1.call-start
  7.2 0.7 slice.18
  7.9 1.7 collective-permute-start
  9.6 1.1 copy.11
  10.7 0.3 collective-permute-done
  11.0 0.8 constant_dynamic-update-slice_fusion
  11.8 0.3 rev.10
  12.1 0.1 slice.24
  12.2 0.3 reverse.1
  12.4 0.1 slice_bitcast_fusion
  12.5 0.2 copy.12
  12.7 0.2 copy.10
  12.9 18.7 %fusion.4 = f32[1,512,256]{1,0,2:T(1,128)S(1)} fusion(bf16[1,64,384]{1,0,2:T(2,128)(2,1)S(1)} %copy.10, bf16[128,64,512]{2,1,0:T(8,128)(2,1)} %param.4), kind=kOutput, calls=%fused_computation.12 | convolution fusion | flops 2147483648 | bytes 8962048 | tf_op jit(solution)/shard_map/slice | solution.py:23
  31.6 0.3 rev.11
  31.9 0.1 subtract_convert_fusion
  32.0 0.0 copy-start
  32.0 0.5 rev.12
  32.5 19.6 %fusion.2 = f32[128,64,512]{2,1,0:T(8,128)} fusion(bf16[64,1,383]{0,1,2:T(2,128)(2,1)S(1)} %copy.12, bf16[512,1,256]{0,2,1:T(8,128)(2,1)S(1)} %bitcast.15), kind=kOutput, calls=%fused_computation.3 | convolution fusion | flops 2147483648 | bytes 17088384 | tf_op jit(solution)/shard_map/conv_general_dilated | solution.py:15
  52.1 0.0 copy-done
  52.1 0.0 copy-start.1
  52.1 0.0 reduce-scatter.2.cloned.1.call-update
  52.1 0.9 copy-done.1
  53.1 1.3 collective-permute-start.1
  54.4 5.8 %collective-permute-done.1 = bf16[512,128]{0,1:T(8,128)(2,1)S(1)} collective-permute-done((bf16[512,128]{0,1:T(8,128)(2,1)S(1)}, bf16[512,128]{0,1:T(8,128)(2,1)S(1)}, u32[]{:S(2)}, u32[]{:S(2)}) %collective-permute-start.1) | collective-permute-done | bytes 131104 | tf_op jit(solution)/shard_map/ppermute | solution.py:11
  60.2 24.0 %fusion = f32[1,64,256]{1,0,2:T(1,128)S(1)} fusion(bf16[128,64,512]{2,1,0:T(8,128)(2,1)} %param.4, bf16[1,512,384]{1,2,0:T(8,128)(2,1)S(1)} %maximum_bitcast_fusion), kind=kOutput, calls=%fused_computation | convolution fusion | flops 2147483648 | bytes 8847360 | tf_op jit(solution)/shard_map/slice | solution.py:28
  84.3 0.1 copy.15
  84.4 13.1 %all_gather.3 = f32[4,64,256]{2,1,0:T(8,128)S(1)} all-gather(f32[1,64,256]{2,1,0:T(8,128)S(1)} %copy.15), channel_id=1, replica_groups=mesh['tm'=64,'neur'=4] {'neur'}, dimensions={0}, use_global_device_ids=true | all-gather | bytes 327680 | tf_op jit(solution)/shard_map/all_gather | solution.py:56
  97.5 0.1 copy.19
  97.6 0.7 copy.17
  98.3 409.9 %reduce-scatter.2.cloned.1.call-done = f32[2,64,512]{2,1,0:T(8,128)} async-done(((f32[128,64,512]{2,1,0:T(8,128)}), f32[2,64,512]{2,1,0:T(8,128)}) %reduce-scatter.2.cloned.1.call-update) | async-done | bytes 262160 | tf_op jit(solution)/shard_map/reduce_scatter | solution.py:62
  508.2 1.7 broadcast_multiply_fusion
  (6 shorter events, 0.1 us)
Async XLA Ops:
  7.2 501.0 %reduce-scatter.2.cloned.1.call-start = ((), (), s32[]{:S(2)}) async-start(), calls=%async_computation.1 | async-start | bytes 17039360 | tf_op jit(solution)/shard_map/reduce_scatter | solution.py:62
  7.9 3.1 collective-permute-start
  32.0 20.1 %copy-start = (bf16[512,256]{0,1:T(8,128)(2,1)}, bf16[512,256]{0,1:T(8,128)(2,1)S(1)}, u32[]{:S(2)}) copy-start(bf16[512,256]{0,1:T(8,128)(2,1)S(1)} %subtract_convert_fusion) | copy-start | bytes 786436
  52.1 1.0 copy-start.1
  53.1 7.1 %collective-permute-start.1 = (bf16[512,128]{0,1:T(8,128)(2,1)S(1)}, bf16[512,128]{0,1:T(8,128)(2,1)S(1)}, u32[]{:S(2)}, u32[]{:S(2)}) collective-permute-start(bf16[512,128]{0,1:T(8,128)(2,1)S(1)} %slice.25), channel_id=1, source_target_pairs={{4,0},{8,4},{12,8},{16,12},{20,16},{24,20},{28,24},{32,28},{36,32}... | collective-permute-start | bytes 393224 | tf_op jit(solution)/shard_map/ppermute | solution.py:11
Sparse Core Ops, SparseCore 0:
  52.3 455.8 reduce-scatter.1
